TPU v7x, 32 devices: a whole 2x2x4 slice. The times are simulated.
32 devices in a mesh: sub: 16 (over z, y, core), lm: 2 (over x).
Axes of the slice: x: 2, y: 2, z: 4, core: 2. Of those that a mesh axis runs over, the one named last changes fastest.
Arguments:
- jacobian: bfloat16 [16, 8, 384, 128], P('sub', 'lm'), may hold values from -0.30618622 to 0.30618622
- camera_block: int32 [16, 8], P('sub', 'lm'), may hold values from 0 to 8
- landmark_block: int32 [16, 8], P('sub', 'lm'), may hold values from 9 to 17
Outputs:
- factors: float32 [3, 32, 252, 576], P(None, ('sub', 'lm'))
- top_front: float32 [2, 32, 36, 1152], P(None, ('sub', 'lm'))
Inputs may be any that keep to these rules, and one draw needn't show every extreme that they name: `camera_block`: camera parts lie in the first half of a front's unknowns. `landmark_block`: landmark parts lie in the second half of a front's unknowns.
All inputs are finite; a program needn't handle non-finite values.
Results may differ from a plain program's by a relative error of at most 0.0003.
Values may be sent and summed in bfloat16 or wider, within the bound.
No kernel may reach another device: no remote copies, remote signals or barrier semaphores. Data moves between devices by JAX's collectives and lax.ppermute only.
A program may use at most 64 MiB of HBM per device.

v0:
```python
import functools

import jax
import jax.numpy as jnp
from jax import lax
from jax.experimental import pallas as pl
from jax.experimental.pallas import tpu as pltpu
from jax.sharding import PartitionSpec as P

BW = 64
F = 1152
LEVELS = 3
E = 576
NB = E // BW
EP = 640
DAMPING = 1.0
f32 = jnp.float32
bf16 = jnp.bfloat16


def iota(shape, axis):
    return lax.broadcasted_iota(jnp.int32, shape, axis)


def row_of(x, t):
    return jnp.broadcast_to(x[t : t + 1, :], x.shape)


def col_of(x, j):
    return jnp.broadcast_to(x[:, j : j + 1], x.shape)


def split2(x):
    hi = x.astype(bf16)
    return hi, (x - hi.astype(f32)).astype(bf16)


def left3(dup):
    hi, lo = split2(dup)
    return jnp.concatenate([hi, lo[:, :64]], axis=1)


def right3(x):
    hi, lo = split2(x)
    return jnp.concatenate([hi, lo, hi], axis=0)


def dot(a, b):
    return jnp.dot(a, b, preferred_element_type=f32)


def dot_nt(a, b):
    return lax.dot_general(a, b, (((1,), (1,)), ((), ())), preferred_element_type=f32)


def roll64(x):
    return pltpu.roll(x, 64, 1)


def factor(mats):
    sub = iota((8, 128), 0)
    zero = [m[0] - m[0] for m in mats]

    def spread(b, x, kb):
        return [col_of(x, 8 * kb + t) + zero[b] for t in range(8)]

    ready = [spread(b, m[0], 0) for b, m in enumerate(mats)]
    for kb in range(8):
        state, below = [], []
        for b, m in enumerate(mats):
            parts = [spread(b, m[v], kb) if v == kb + 1 else [col_of(m[v], 8 * kb + t) for t in range(8)] for v in range(kb + 1, 8)]
            below.append(parts)
            coming = spread(b, m[kb + 1], kb + 1) if kb < 7 else []
            ahead = list(parts[0]) if kb < 7 else []
            state.append([m[kb], m[kb], ready[b], jnp.ones((8, 128), f32), jnp.ones((8, 128), f32), ahead, coming])
        for t in range(8):
            for st in state:
                fwd, both, cols, diag, recip, ahead, coming = st
                col = cols[t]
                d = row_of(col, t)
                rd = 1.0 / d
                st[3] = jnp.where(sub == t, d, diag)
                st[4] = jnp.where(sub == t, rd, recip)
                mult = jnp.where(sub == t, 0.0, col * rd)
                for t2 in range(t + 1, 8):
                    cols[t2] = cols[t2] - mult * row_of(cols[t2], t)
                st[1] = both - mult * row_of(both, t)
                st[0] = fwd - jnp.where(sub > t, mult, 0.0) * row_of(fwd, t)
                if ahead:
                    weight = ahead[t]
                    scaled = weight * rd
                    for t2 in range(t + 1, 8):
                        ahead[t2] = ahead[t2] - scaled * row_of(col, t2)
                    for t2 in range(8):
                        coming[t2] = coming[t2] - weight * row_of(scaled, t2)
        for b, m in enumerate(mats):
            fwd, both, cols, diag, recip, ahead, coming = state[b]
            m[kb] = fwd * lax.rsqrt(diag)
            solved = both * recip
            rows = [row_of(solved, t) for t in range(8)]
            for v in range(kb + 1, 8):
                terms = [below[b][v - kb - 1][t] * rows[t] for t in range(8)]
                while len(terms) > 1:
                    terms = [x + y for x, y in zip(terms[0::2], terms[1::2])]
                m[v] = m[v] - terms[0]
            ready[b] = coming
    return mats


def augmented(x):
    lane, row = iota((64, 128), 1), iota((64, 128), 0)
    full = jnp.where(lane < 64, x, jnp.where(lane - 64 == row, 1.0, 0.0))
    return [full[8 * v : 8 * v + 8] for v in range(8)]


def joined(rows):
    return jnp.concatenate(rows, axis=0)


def tiles_kernel(cam_ref, lm_ref, jac_ref, pay_ref, sum_ref):
    lane = iota((64, 128), 1)
    blocks = jac_ref.shape[0]
    sum_ref[...] = jnp.zeros_like(sum_ref)
    lane8, row8 = iota((8, 128), 1), iota((8, 128), 0)
    row, col = iota((64, 128), 0), lane % 64
    index = jnp.zeros((8, 128), f32)
    tops, lls = [], []
    for n in range(blocks):
        j = jac_ref[n]
        t = lax.dot_general(j, j, (((0,), (0,)), ((), ())), preferred_element_type=f32)
        top = t[:64]
        tops.append(top)
        lls.append(t[64:])
        c = cam_ref[n]
        cc = jnp.where(lane < 64, top, roll64(top))
        mine = (lane >= 64).astype(jnp.int32) == c % 2
        at = pl.ds(pl.multiple_of(c // 2 * 64, 64), 64)
        sum_ref[at, :] = sum_ref[at, :] + jnp.where(mine, cc, 0.0)
        index = jnp.where((lane8 == n) & (row8 == 0), c.astype(f32), index)
        index = jnp.where((lane8 == n) & (row8 == 1), lm_ref[n].astype(f32), index)
    for k in range(blocks // 2):
        both = jnp.where(lane < 64, roll64(tops[2 * k]), tops[2 * k + 1])
        pay_ref[64 * k : 64 * k + 64, :] = both
    for k in range(blocks // 4):
        first = jnp.where(lane < 64, roll64(lls[4 * k]), lls[4 * k + 2])
        second = jnp.where(lane < 64, roll64(lls[4 * k + 1]), lls[4 * k + 3])
        base = 64 * (blocks // 2 + k)
        pay_ref[base : base + 64, :] = jnp.where(row >= col, first, second)
        diag = jnp.sum(jnp.where(row == col, second, 0.0), axis=0, keepdims=True)
        index = jnp.where(row8 == 2 + k, jnp.broadcast_to(diag, (8, 128)), index)
    pay_ref[64 * (3 * blocks // 4) :, :] = index


def bottom_kernel(info_ref, cam_ref, sum_a, sum_b, pay_ref, out_ref, own_ref, w_ref, v_ref):
    lane, row = iota((64, 128), 1), iota((64, 128), 0)
    own_ref[...] = jnp.zeros_like(own_ref)
    together = 3

    def several(g, carry):
        mats = []
        for i in range(together):
            c = g * together + i
            at = pl.ds(pl.multiple_of(c // 2 * 64, 64), 64)
            x = sum_a[at, :] + sum_b[at, :]
            x = jnp.where(c % 2 == 1, roll64(x), x)
            mats.append(augmented(x + jnp.where(lane == row, 2 * DAMPING, 0.0)))
        mats = factor(mats)
        for i in range(together):
            v_ref[g * together + i] = joined(mats[i])
        return carry

    lax.fori_loop(0, NB // together, several, 0)
    spread = info_ref[4]
    place = info_ref[1]
    count = own_ref.shape[1] // NB
    pick = (iota((128, count), 0) == iota((128, count), 1) * spread + place).astype(bf16)
    for c in range(NB):
        v = v_ref[c]
        w = roll64(v)
        w_ref[c] = left3(jnp.where(lane < 64, w, v))
        upper = jnp.where((lane >= row) & (lane < 64), v, 0.0)
        hi, lo = split2(upper)
        own_ref[64 * c : 64 * c + 64, count * c : count * c + count] = dot(hi, pick) + dot(lo, pick)
    blocks = cam_ref.shape[0]
    for k in range(blocks // 2):
        x = pay_ref[64 * k : 64 * k + 64, :]
        xr = roll64(x)
        y0 = dot(w_ref[cam_ref[2 * k]], right3(jnp.where(lane < 64, x, xr)))
        y1 = dot(w_ref[cam_ref[2 * k + 1]], right3(jnp.where(lane < 64, xr, x)))
        out_ref[64 * k : 64 * k + 64, :] = jnp.where(lane < 64, y0, y1)
    out_ref[32 * blocks :, :] = pay_ref[32 * blocks :, :]


def climb(a_ref, w_ref, n_ref, l_ref, r_ref, batch):
    lane64 = iota((64, 128), 1)
    width = a_ref.shape[2]

    def keep_inverse(b, mat):
        v = joined(mat)
        hi, lo = split2(jnp.where(lane64 < 64, roll64(v), v))
        w_ref[b] = jnp.concatenate([hi, lo[:, :64]], axis=1)
        n = jnp.concatenate([jnp.where(lane64 < 64, hi, lo), hi[:, :64]], axis=1)
        n_ref[b] = jnp.concatenate([n, n], axis=0)

    def finish(b, w, at, j):
        u = dot(w, right3(a_ref[b, at, :]))
        keep = iota((64, EP), 1) >= j * 64 + iota((64, EP), 0)
        us = jnp.where(keep, u[:, :EP], 0.0)
        a_ref[b, at, 0:EP] = us
        a_ref[b, at, EP:] = u[:, EP:]
        return us, u

    mats = factor([augmented(a_ref[b, 0:64, 0:128]) for b in range(batch)])
    for b in range(batch):
        keep_inverse(b, mats[b])

    for first, last in ((1, 4), (4, 7), (7, 9)):
        low_row = 64 * first
        low_lane = low_row // 128 * 128
        starts = [low_lane] + list(range(EP, width, EP))
        sizes = [EP - low_lane] + [EP] * (len(starts) - 1)

        def step(j, carry, low_row=low_row, starts=starts, sizes=sizes):
            at = pl.ds(pl.multiple_of(j * 64 - 64, 64), 64)
            rows = pl.ds(pl.multiple_of(j * 64, 64), 64)
            wide = pl.ds(pl.multiple_of(j // 2 * 128, 128), 128)
            narrow = pl.ds(pl.multiple_of((j - 1) // 2 * 128, 128), 128)
            odd = j % 2 == 1
            olds = [w_ref[b] for b in range(batch)]
            mats = []
            for b in range(batch):
                us = dot(olds[b], right3(a_ref[b, at, wide]))
                us = jnp.where(odd, roll64(us), us)
                side = a_ref[b, rows, narrow]
                turned = roll64(side)
                side = jnp.where((lane64 < 64) == odd, side, turned)
                left = left3(-dot_nt(left3(side), n_ref[b]))
                x = a_ref[b, rows, wide]
                x = jnp.where(odd, roll64(x), x)
                mats.append(augmented(x + dot(left, right3(us))))
            mats = factor(mats)
            for b in range(batch):
                us, u = finish(b, olds[b], at, j - 1)
                xs = jnp.where(iota((64, EP), 1) >= j * 64, -us, 0.0)
                l_ref[b] = left3(jnp.concatenate([xs, xs], axis=0).T)
                r_ref[b] = right3(u)
                left = l_ref[b, low_row:E]
                for s, size in zip(starts, sizes):
                    a_ref[b, low_row:E, s : s + size] = a_ref[b, low_row:E, s : s + size] + dot(
                        left, r_ref[b, :, s : s + size]
                    )
            for b in range(batch):
                keep_inverse(b, mats[b])
            return carry

        lax.fori_loop(first, last, step, 0)
    for b in range(batch):
        finish(b, w_ref[b], slice(E - 64, E), NB - 1)


def gram_left(u, left_ref):
    hi, lo = split2((-u).T)
    left_ref[:, 0:EP] = hi
    left_ref[:, EP : 2 * EP] = hi
    left_ref[:, 2 * EP :] = lo


def spread_lanes(pick, u):
    hi, lo = split2(u)
    return dot(hi, pick) + dot(lo, pick)


def minus_rows(rows, u):
    count = rows.shape[0]
    hi, lo = split2(-rows)
    uh, ul = split2(u)
    both = dot(jnp.concatenate([hi, lo], axis=0), uh)
    return both[:count] + both[count:] + dot(hi, ul)


def upper_kernel(nslots, blocks, lm_count_static, info_ref, *refs):
    pays = refs[:nslots]
    own0_ref, fac_ref, top_ref = refs[nslots : nslots + 3]
    (all_ref, ivm, ism, sem, ydup, tbuf, lbuf, own_u0, odd_up, a1, a2, pri) = refs[nslots + 3 : nslots + 15]
    (w_ref, n_ref, l_ref, r_ref, left_ref, right_ref) = refs[nslots + 15 :]
    lane, row = iota((64, 128), 1), iota((64, 128), 0)
    col = lane % 64
    me, my_lm = info_ref[0], info_ref[5]
    lm_count = lm_count_static
    per = blocks * nslots // 8

    for slot in range(nslots):
        s = me ^ (slot // 2)
        spot = s * 2 + (my_lm ^ (slot % 2))
        tail = pays[slot][48 * blocks : 48 * blocks + 8, :]
        ivm[pl.ds(pl.multiple_of(spot * 8, 8), 8), :] = tail.astype(jnp.int32)
        for k in range(blocks // 4):
            base = 64 * (blocks // 2 + k)
            packed = pays[slot][base : base + 64, :]
            turned = jnp.concatenate([packed, packed], axis=0).T
            turned = jnp.where(lane < 64, turned[0:64], turned[64:128])
            diag = jnp.broadcast_to(tail[2 + k : 3 + k, :], (64, 128))
            first = jnp.where(row >= col, packed, turned)
            second = jnp.where(row < col, packed, jnp.where(row > col, turned, diag))
            for i in range(2):
                y = pays[slot][64 * (2 * k + i) : 64 * (2 * k + i) + 64, :]
                yr = roll64(y)
                for h, ll in enumerate((first, second)):
                    at = pl.ds(pl.multiple_of((spot * blocks + 4 * k + 2 * i + h) * 64, 64), 64)
                    ll = ll if i else roll64(ll)
                    all_ref[at, :] = jnp.where(lane < 64, yr if h else y, ll)
    copy = pltpu.make_async_copy(ivm, ism, sem)
    copy.start()
    eye2 = jnp.where(iota((E, EP), 0) == iota((E, EP), 1), 2 * DAMPING, 0.0)
    own_u0[...] = jnp.zeros_like(own_u0)
    odd_up[...] = jnp.zeros_like(odd_up)
    for m in range(2):
        a1[m] = jnp.zeros(a1.shape[1:], f32)
        a1[m, 0:E, 0:EP] = eye2
        for v in range(EP // 128):
            pri[m * (EP // 128) + v] = 0.5 * eye2[:, 128 * v : 128 * v + 128]
    a2[0, 0:E, 0:EP] = eye2
    copy.wait()

    def ids(s, k):
        row = (s * 2 + k // blocks) * 8
        return ism[row, k % blocks], ism[row + 1, k % blocks]

    def rows64(i):
        return pl.ds(pl.multiple_of(i * 64, 64), 64)

    def lanes128(i):
        return pl.ds(pl.multiple_of(i * 128, 128), 128)

    def dups(s, k):
        x = all_ref[rows64(s * per + k), :]
        xr = roll64(x)
        return jnp.where(lane < 64, x, xr), jnp.where(lane < 64, xr, x)

    def half_of(l):
        return (lane >= 64).astype(jnp.int32) == l % 2

    for s in range(8):
        pair, half, merge = s // 2, s % 2, s // 4
        second = pair % 2

        def place(k, carry, s=s, pair=pair, half=half, merge=merge, second=second):
            c, l = ids(s, k)
            y, ll = dups(s, k)
            mine = half_of(l)
            ydup[pair, :, lanes128(half * per + k)] = y
            rows, lanes = rows64(l), lanes128(l // 2)
            ll = jnp.where(mine, ll, 0.0)
            if half == 0:
                a1[merge, rows, lanes] = a1[merge, rows, lanes] + ll
            elif second == 0:
                a2[0, rows, lanes] = a2[0, rows, lanes] + ll
            else:
                tile = merge * (EP // 128) + l // 2
                pri[tile, rows, :] = pri[tile, rows, :] + ll
                odd_up[merge, rows64(c), lanes] = odd_up[merge, rows64(c), lanes] + jnp.where(mine, y, 0.0)
            return carry

        lax.fori_loop(0, per, place, 0)

    my_pair = me // 2
    for half in range(2):

        def place_own(k, carry, half=half):
            c, l = ids(2 * my_pair + half, k)
            y, _ = dups(2 * my_pair + half, k)
            lanes = lanes128(half * (EP // 128) + l // 2)
            own_u0[rows64(c), lanes] = own_u0[rows64(c), lanes] + jnp.where(half_of(l), y, 0.0)
            return carry

        lax.fori_loop(0, per, place_own, 0)

    def gram_pair(p, carry):
        merge = p // 2

        def transposed(first):
            for k in range(per):
                t = ydup[p, :, 128 * (first + k) : 128 * (first + k + 1)]
                tt = jnp.concatenate([t, t], axis=0).T
                lbuf[64 * k : 64 * k + 64, :] = left3(-tt[0:64])

        def scatter(target, s_rows, halves, base):
            def body(n, carry):
                cn, ln = ids(s_rows, n)
                for i, h in enumerate(halves):
                    for k in range(per):
                        ck, lk = ids(2 * p + h, k)

                        @pl.when(ck == cn)
                        def _():
                            got = tbuf[rows64(n), 128 * (i * per + k) : 128 * (i * per + k + 1)]
                            to = pl.ds(pl.multiple_of(base[h] + lk // 2 * 128, 128), 128)
                            view = target.at[rows64(ln), to]
                            view[...] = view[...] + jnp.where(half_of(lk), got, 0.0)

                return carry

            lax.fori_loop(0, per, body, 0)

        transposed(0)
        wide = 128 * per
        for h in range(2):
            tbuf[:, h * wide : h * wide + wide] = dot(lbuf[...], right3(ydup[p, :, h * wide : h * wide + wide]))
        scatter(a1.at[merge], 2 * p, (0, 1), (0, EP + p % 2 * EP))

        @pl.when(p % 2 == 0)
        def _():
            transposed(per)
            tbuf[:, 0:wide] = dot(lbuf[...], right3(ydup[p, :, wide : 2 * wide]))
            scatter(a2.at[0], 2 * p + 1, (1,), (0, 0))

        return carry

    lax.fori_loop(0, 4, gram_pair, 0)

    climb(a1, w_ref, n_ref, l_ref, r_ref, 2)

    def gram_merge(m, carry):
        u = a1[m, :, EP : 3 * EP]
        hi, lo = split2(u)
        right_ref[0:EP] = hi
        right_ref[EP : 2 * EP] = lo
        right_ref[2 * EP :] = hi
        gram_left(u[:, 0:EP], left_ref)
        a2[0, 0:E, 0:EP] = a2[0, 0:E, 0:EP] + dot(left_ref[0:E], right_ref[:, 0:EP])
        to = pl.ds(pl.multiple_of(EP + m * EP, 128), EP)
        a2[0, 0:E, to] = dot(left_ref[0:E], right_ref[:, EP : 2 * EP])
        return carry

    lax.fori_loop(0, 2, gram_merge, 0)

    climb(a2, w_ref, n_ref, l_ref, r_ref, 1)

    def pick_of(count, spread, place):
        return (iota((EP, count), 0) == iota((EP, count), 1) * spread + place).astype(bf16)

    n0 = own0_ref.shape[1]
    n1, n2 = n0 // 2, n0 // 4
    merge = me // 4
    pick0 = pick_of(n0, 2 * lm_count, info_ref[1])
    pick1 = pick_of(n1, 4 * lm_count, info_ref[2])
    pick2 = pick_of(n2, 8 * lm_count, info_ref[3])
    fac_ref[0, :, 0:n0] = own0_ref[...]
    fac_ref[1, :, 0:n0] = spread_lanes(pick0, own_u0[:, 0:EP])
    fac_ref[2, :, 0:n0] = spread_lanes(pick0, own_u0[:, EP : 2 * EP])
    for t in range(3):
        fac_ref[t, :, n0 : n0 + n1] = spread_lanes(pick1, a1[merge, 0:E, t * EP : t * EP + EP])
    fac_ref[0, :, n0 + n1 : n0 + n1 + n2] = spread_lanes(pick2, a2[0, 0:E, 0:EP])

    def both_halves(low, up):
        r, c = iota((EP, 128), 0), iota((EP, 128), 1)
        source = c % 64 * (8 * lm_count) + info_ref[3]
        hit = (r == source) & (c % 64 < n2)
        at0 = (hit & (c < 64)).astype(bf16)
        at1 = (hit & (c >= 64)).astype(bf16)
        return spread_lanes(at0, low) + spread_lanes(at1, up)

    got = both_halves(a2[0, 0:E, EP : 2 * EP], a2[0, 0:E, 2 * EP : 3 * EP])
    fac_ref[1, :, n0 + n1 : n0 + n1 + n2] = got[:, 0:n2]
    fac_ref[2, :, n0 + n1 : n0 + n1 + n2] = got[:, 64 : 64 + n2]
    part = minus_rows(got.T, a2[0, 0:E, EP : 3 * EP])
    rows0 = both_halves(odd_up[0], odd_up[1]).T
    rows1 = both_halves(a1[0, 0:E, 2 * EP : 3 * EP], a1[1, 0:E, 2 * EP : 3 * EP]).T
    for h in range(2):
        own = minus_rows(rows0[64 * h : 64 * h + 64], odd_up[h])
        own = own + minus_rows(rows1[64 * h : 64 * h + 64], a1[h, 0:E, 2 * EP : 3 * EP])
        mine = pl.ds(info_ref[3], n2, stride=8 * lm_count)
        kept = [pri[h * (EP // 128) + v, mine, :] for v in range(EP // 128)]
        own = own[0:n2] + jnp.concatenate(kept, axis=1)
        for g in range(2):
            value = part[64 * h : 64 * h + n2, g * EP : g * EP + EP]
            if g == h:
                value = value + own
            top_ref[h, :, 0, g * E : g * E + E] = value[:, 0:E]


def vmem(n):
    return [pl.BlockSpec(memory_space=pltpu.VMEM)] * n


def smem(n):
    return [pl.BlockSpec(memory_space=pltpu.SMEM)] * n


LIMIT = 60 * 1024 * 1024


def local(jacobian, camera_block, landmark_block):
    lm_count = lax.axis_size("lm")
    sub_count = lax.axis_size("sub")
    lm_place = lax.axis_index("lm")
    sub_place = lax.axis_index("sub")
    group = 2**LEVELS
    jac = jacobian[0]
    blocks = jac.shape[0]

    def swap(value, sub_mask, lm_mask):
        pairs = [
            (s * lm_count + l, (s ^ sub_mask) * lm_count + (l ^ lm_mask))
            for s in range(sub_count)
            for l in range(lm_count)
        ]
        return lax.ppermute(value, ("sub", "lm"), pairs)

    info = jnp.stack(
        [
            sub_place % group,
            sub_place % 2 * lm_count + lm_place,
            sub_place % 4 * lm_count + lm_place,
            sub_place % 8 * lm_count + lm_place,
            jnp.int32(2 * lm_count),
            lm_place,
        ]
    ).astype(jnp.int32)
    cams = camera_block[0]
    lms = landmark_block[0] - NB
    payload = jax.ShapeDtypeStruct((48 * blocks + 8, 128), f32)

    pay, sums = pl.pallas_call(
        tiles_kernel,
        out_shape=(payload, jax.ShapeDtypeStruct(((NB + 1) // 2 * 64, 128), f32)),
        in_specs=smem(2) + vmem(1),
        out_specs=tuple(vmem(2)),
    )(cams, lms, jac)
    half_sums = sums + swap(sums, 1, 0)
    other_sums = swap(half_sums, 0, 1)

    count0 = E // (2 * lm_count)
    pay, own0 = pl.pallas_call(
        bottom_kernel,
        out_shape=(payload, jax.ShapeDtypeStruct((E, count0), f32)),
        in_specs=smem(2) + vmem(3),
        out_specs=tuple(vmem(2)),
        scratch_shapes=[pltpu.VMEM((NB, 64, 192), bf16), pltpu.VMEM((NB, 64, 128), f32)],
    )(info, cams, half_sums, other_sums, pay)

    held = {(0, 0): pay}
    for sub_mask, lm_mask in ((0, 1), (2, 0), (4, 0), (1, 0)):
        held.update({(q ^ sub_mask, l ^ lm_mask): swap(v, sub_mask, lm_mask) for (q, l), v in held.items()})
    slots = [held[q, l] for q in range(group) for l in range(2)]
    nslots = len(slots)
    per = blocks * 2
    factors, top = pl.pallas_call(
        functools.partial(upper_kernel, nslots, blocks, lm_count),
        out_shape=(
            jax.ShapeDtypeStruct((3, E, count0 * 7 // 4), f32),
            jax.ShapeDtypeStruct((2, count0 // 4, 1, F), f32),
        ),
        in_specs=smem(1) + vmem(nslots + 1),
        out_specs=tuple(vmem(2)),
        scratch_shapes=[
            pltpu.VMEM((nslots * blocks * 64, 128), f32),
            pltpu.VMEM((nslots * 8, 128), jnp.int32),
            pltpu.SMEM((nslots * 8, 128), jnp.int32),
            pltpu.SemaphoreType.DMA(()),
            pltpu.VMEM((4, 64, 2 * per * 128), f32),
            pltpu.VMEM((per * 64, 2 * per * 128), f32),
            pltpu.VMEM((per * 64, 192), bf16),
            pltpu.VMEM((E, 2 * EP), f32),
            pltpu.VMEM((2, E, EP), f32),
            pltpu.VMEM((2, EP, 3 * EP), f32),
            pltpu.VMEM((1, EP, 3 * EP), f32),
            pltpu.VMEM((2 * (EP // 128), E, 128), f32),
            pltpu.VMEM((2, 64, 192), bf16),
            pltpu.VMEM((2, 128, 192), bf16),
            pltpu.VMEM((2, EP, 192), bf16),
            pltpu.VMEM((2, 192, 3 * EP), bf16),
            pltpu.VMEM((EP, 3 * EP), bf16),
            pltpu.VMEM((3 * EP, 2 * EP), bf16),
        ],
        compiler_params=pltpu.CompilerParams(vmem_limit_bytes=LIMIT),
    )(info, *slots, own0)
    return jnp.transpose(factors, (0, 2, 1))[:, None], jnp.transpose(top, (0, 2, 1, 3))


def solution(mesh):
    placed = (P("sub", "lm", None, None), P("sub", "lm"), P("sub", "lm"))
    return jax.shard_map(
        local,
        mesh=mesh,
        in_specs=placed,
        out_specs=(P(None, ("sub", "lm"), None, None), P(None, ("sub", "lm"), None, None)),
        check_vma=False,
    )
```

profile of v0, /device:TPU:0, one launch (start us, length us, event | category | flops | bytes accessed | tf_op | source)
XLA Modules:
  0.0 125.0 jit_solution(10807178958836134565)
XLA Ops:
  0.6 1.2 add_bitcast_fusion.lm_ref
  1.8 2.1 %shard_map.50 = (f32[200,128]{1,0:T(8,128)}, f32[320,128]{1,0:T(8,128)}) custom-call(s32[4]{0:T(128)} %bitcast.16, s32[4]{0:T(128)} %add_bitcast_fusion.lm_ref, bf16[4,384,128]{2,1,0:T(8,128)(2,1)} %bitcast.15), custom_call_target="tpu_custom_call" | custom-call | tf_op jit(solution)/shard_map/pallas_call | solution.py:524
  3.9 0.5 collective-permute-start
  4.3 1.2 collective-permute-done
  5.6 0.9 add.31.sum_a
  6.5 0.0 copy-start
  6.5 2.9 %collective-permute-start.1 = (f32[320,128]{1,0:T(8,128)S(1)}, f32[320,128]{1,0:T(8,128)S(1)}, u32[]{:S(2)}, u32[]{:S(2)}) collective-permute-start(f32[320,128]{1,0:T(8,128)S(1)} %add.31.sum_a), channel_id=1, source_target_pairs={{0,1},{1,0},{2,3},{3,2},{4,5},{5,4},{6,7},{7,6},{8,9},{9,8},{10,11... | collective-permute-start | bytes 491528 | tf_op jit(solution)/shard_map/ppermute | solution.py:508
  9.5 0.6 stack.23.info_ref
  10.1 3.9 %collective-permute-done.1.sum_b = f32[320,128]{1,0:T(8,128)S(1)} collective-permute-done((f32[320,128]{1,0:T(8,128)S(1)}, f32[320,128]{1,0:T(8,128)S(1)}, u32[]{:S(2)}, u32[]{:S(2)}) %collective-permute-start.1) | collective-permute-done | bytes 163872 | tf_op jit(solution)/shard_map/ppermute | solution.py:508
  14.0 0.0 copy-start.1
  14.0 0.0 copy-done
  14.0 0.7 copy-done.1
  14.6 8.8 %shard_map.51 = (f32[200,128]{1,0:T(8,128)}, f32[576,144]{1,0:T(8,128)}) custom-call(s32[6]{0:T(128)} %stack.23.info_ref, s32[4]{0:T(128)} %bitcast.17, f32[320,128]{1,0:T(8,128)} %copy-done, f32[320,128]{1,0:T(8,128)} %copy-done.1, f32[200,128]{1,0:T(8,128)} %get-tuple-element.9.pay_ref), custom_call_target="tpu_custom_call" | custom-call | tf_op jit(solution)/shard_map/pallas_call | solution.py:534
  23.4 1.7 %collective-permute-start.2 = (f32[200,128]{1,0:T(8,128)}, f32[200,128]{1,0:T(8,128)S(1)}, u32[]{:S(2)}, u32[]{:S(2)}) collective-permute-start(f32[200,128]{1,0:T(8,128)} %get-tuple-element.10.refs_0_), channel_id=1, source_target_pairs={{0,1},{1,0},{2,3},{3,2},{4,5},{5,4},{6,7},{7,6},{8,9},{9,8},{10,11... | collective-permute-start | bytes 307208 | tf_op jit(solution)/shard_map/ppermute | solution.py:508
  25.1 1.6 %collective-permute-start.9 = (f32[200,128]{1,0:T(8,128)}, f32[200,128]{1,0:T(8,128)S(1)}, u32[]{:S(2)}, u32[]{:S(2)}) collective-permute-start(f32[200,128]{1,0:T(8,128)} %get-tuple-element.10.refs_0_), channel_id=1, source_target_pairs={{0,8},{1,9},{2,10},{3,11},{4,12},{5,13},{6,14},{7,15},{8,0},{9,1},... | collective-permute-start | bytes 307208 | tf_op jit(solution)/shard_map/ppermute | solution.py:508
  26.7 1.5 %collective-permute-start.5 = (f32[200,128]{1,0:T(8,128)}, f32[200,128]{1,0:T(8,128)S(1)}, u32[]{:S(2)}, u32[]{:S(2)}) collective-permute-start(f32[200,128]{1,0:T(8,128)} %get-tuple-element.10.refs_0_), channel_id=1, source_target_pairs={{0,4},{1,5},{2,6},{3,7},{4,0},{5,1},{6,2},{7,3},{8,12},{9,13},{10,... | collective-permute-start | bytes 307208 | tf_op jit(solution)/shard_map/ppermute | solution.py:508
  28.2 0.0 collective-permute-start.3
  28.2 0.0 collective-permute-done.2.refs_1_
  28.3 0.0 copy-start.2
  28.3 1.8 %collective-permute-start.6 = (f32[200,128]{1,0:T(8,128)S(1)}, f32[200,128]{1,0:T(8,128)S(1)}, u32[]{:S(2)}, u32[]{:S(2)}) collective-permute-start(f32[200,128]{1,0:T(8,128)S(1)} %collective-permute-done.2.refs_1_), channel_id=1, source_target_pairs={{0,4},{1,5},{2,6},{3,7},{4,0},{5,1},{6,2},{7,3},{8,12},{9,13},{10,... | collective-permute-start | bytes 307208 | tf_op jit(solution)/shard_map/ppermute | solution.py:508
  30.0 0.0 collective-permute-done.9.refs_8_
  30.0 0.0 copy-start.3
  30.0 0.0 collective-permute-start.11
  30.0 1.8 %collective-permute-done.5.refs_4_ = f32[200,128]{1,0:T(8,128)S(1)} collective-permute-done((f32[200,128]{1,0:T(8,128)}, f32[200,128]{1,0:T(8,128)S(1)}, u32[]{:S(2)}, u32[]{:S(2)}) %collective-permute-start.5) | collective-permute-done | bytes 102432 | tf_op jit(solution)/shard_map/ppermute | solution.py:508
  31.8 0.4 collective-permute-start.13
  32.3 0.0 collective-permute-start.7
  32.3 0.0 collective-permute-done.3.refs_2_
  32.3 1.6 %collective-permute-start.10 = (f32[200,128]{1,0:T(8,128)S(1)}, f32[200,128]{1,0:T(8,128)S(1)}, u32[]{:S(2)}, u32[]{:S(2)}) collective-permute-start(f32[200,128]{1,0:T(8,128)S(1)} %collective-permute-done.2.refs_1_), channel_id=1, source_target_pairs={{0,8},{1,9},{2,10},{3,11},{4,12},{5,13},{6,14},{7,15},{8,0},{9,1},... | collective-permute-start | bytes 307208 | tf_op jit(solution)/shard_map/ppermute | solution.py:508
  33.9 0.0 collective-permute-done.6.refs_5_
  33.9 0.8 collective-permute-start.14
  34.8 0.0 collective-permute-done.11.refs_10_
  34.8 0.0 collective-permute-start.4
  34.8 2.8 %collective-permute-done.13.refs_12_ = f32[200,128]{1,0:T(8,128)S(1)} collective-permute-done((f32[200,128]{1,0:T(8,128)S(1)}, f32[200,128]{1,0:T(8,128)S(1)}, u32[]{:S(2)}, u32[]{:S(2)}) %collective-permute-start.13) | collective-permute-done | bytes 102432 | tf_op jit(solution)/shard_map/ppermute | solution.py:508
  37.6 0.0 collective-permute-start.8
  37.6 0.0 collective-permute-done.7.refs_6_
  37.6 0.0 copy-start.9
  37.6 0.5 collective-permute-start.15
  38.1 1.7 %collective-permute-done.10.refs_9_ = f32[200,128]{1,0:T(8,128)S(1)} collective-permute-done((f32[200,128]{1,0:T(8,128)S(1)}, f32[200,128]{1,0:T(8,128)S(1)}, u32[]{:S(2)}, u32[]{:S(2)}) %collective-permute-start.10) | collective-permute-done | bytes 102432 | tf_op jit(solution)/shard_map/ppermute | solution.py:508
  39.8 0.0 collective-permute-start.12
  39.8 1.1 collective-permute-done.14.refs_13_
  40.9 0.0 collective-permute-start.16
  40.9 0.0 collective-permute-done.4.refs_3_
  40.9 0.0 copy-start.12
  40.9 0.0 collective-permute-done.15.refs_14_
  40.9 0.0 copy-start.14
  40.9 0.2 collective-permute-done.12.refs_11_
  41.1 0.0 collective-permute-done.8.refs_7_
  41.1 1.1 collective-permute-done.16.refs_15_
  42.2 0.0 copy-done.2
  42.2 0.0 copy-done.3
  42.2 0.0 copy-done.4
  42.2 0.0 copy-done.5
  42.2 0.0 copy-done.6
  42.2 0.0 copy-done.7
  42.2 0.0 copy-done.8
  42.2 0.0 copy-done.9
  42.2 0.0 copy-done.10
  42.3 0.0 copy-done.11
  42.3 0.0 copy-done.12
  42.3 0.0 copy-done.14
  42.3 0.0 copy-done.15
  42.3 0.0 copy-done.13
  42.3 0.5 copy-done.16
  42.8 82.0 %shard_map.52 = (f32[3,576,252]{2,1,0:T(8,128)}, f32[2,36,1,1152]{3,2,1,0:T(1,128)}) custom-call(s32[6]{0:T(128)} %stack.23.info_ref, f32[200,128]{1,0:T(8,128)} %get-tuple-element.10.refs_0_, f32[200,128]{1,0:T(8,128)} %copy-done.2, f32[200,128]{1,0:T(8,128)} %copy-done.5, f32[200,128]{1,0:T(8,128)} %copy-done.12, f32[200,128]{1,0:T(8,128)} %copy-done.4, ...), custom_call_target="tpu_custom_call" | custom-call | tf_op jit(solution)/shard_map/pallas_call | solution.py:548
  (10 shorter events, 0.0 us)
Async XLA Ops:
  3.9 1.7 %collective-permute-start = (f32[320,128]{1,0:T(8,128)}, f32[320,128]{1,0:T(8,128)S(1)}, u32[]{:S(2)}, u32[]{:S(2)}) collective-permute-start(f32[320,128]{1,0:T(8,128)} %get-tuple-element.8), channel_id=1, source_target_pairs={{0,2},{1,3},{2,0},{3,1},{4,6},{5,7},{6,4},{7,5},{8,10},{9,11},{10,... | collective-permute-start | bytes 491528 | tf_op jit(solution)/shard_map/ppermute | solution.py:508
  6.5 7.4 %copy-start = (f32[320,128]{1,0:T(8,128)}, f32[320,128]{1,0:T(8,128)S(1)}, u32[]{:S(2)}) copy-start(f32[320,128]{1,0:T(8,128)S(1)} %add.31.sum_a) | copy-start | bytes 491524
  6.5 7.4 %collective-permute-start.1 = (f32[320,128]{1,0:T(8,128)S(1)}, f32[320,128]{1,0:T(8,128)S(1)}, u32[]{:S(2)}, u32[]{:S(2)}) collective-permute-start(f32[320,128]{1,0:T(8,128)S(1)} %add.31.sum_a), channel_id=1, source_target_pairs={{0,1},{1,0},{2,3},{3,2},{4,5},{5,4},{6,7},{7,6},{8,9},{9,8},{10,11... | collective-permute-start | bytes 491528 | tf_op jit(solution)/shard_map/ppermute | solution.py:508
  14.0 0.7 copy-start.1
  23.4 4.9 %collective-permute-start.2 = (f32[200,128]{1,0:T(8,128)}, f32[200,128]{1,0:T(8,128)S(1)}, u32[]{:S(2)}, u32[]{:S(2)}) collective-permute-start(f32[200,128]{1,0:T(8,128)} %get-tuple-element.10.refs_0_), channel_id=1, source_target_pairs={{0,1},{1,0},{2,3},{3,2},{4,5},{5,4},{6,7},{7,6},{8,9},{9,8},{10,11... | collective-permute-start | bytes 307208 | tf_op jit(solution)/shard_map/ppermute | solution.py:508
  25.1 4.9 %collective-permute-start.9 = (f32[200,128]{1,0:T(8,128)}, f32[200,128]{1,0:T(8,128)S(1)}, u32[]{:S(2)}, u32[]{:S(2)}) collective-permute-start(f32[200,128]{1,0:T(8,128)} %get-tuple-element.10.refs_0_), channel_id=1, source_target_pairs={{0,8},{1,9},{2,10},{3,11},{4,12},{5,13},{6,14},{7,15},{8,0},{9,1},... | collective-permute-start | bytes 307208 | tf_op jit(solution)/shard_map/ppermute | solution.py:508
  26.7 5.1 %collective-permute-start.5 = (f32[200,128]{1,0:T(8,128)}, f32[200,128]{1,0:T(8,128)S(1)}, u32[]{:S(2)}, u32[]{:S(2)}) collective-permute-start(f32[200,128]{1,0:T(8,128)} %get-tuple-element.10.refs_0_), channel_id=1, source_target_pairs={{0,4},{1,5},{2,6},{3,7},{4,0},{5,1},{6,2},{7,3},{8,12},{9,13},{10,... | collective-permute-start | bytes 307208 | tf_op jit(solution)/shard_map/ppermute | solution.py:508
  28.2 4.1 %collective-permute-start.3 = (f32[200,128]{1,0:T(8,128)}, f32[200,128]{1,0:T(8,128)S(1)}, u32[]{:S(2)}, u32[]{:S(2)}) collective-permute-start(f32[200,128]{1,0:T(8,128)} %get-tuple-element.10.refs_0_), channel_id=1, source_target_pairs={{0,2},{1,3},{2,0},{3,1},{4,6},{5,7},{6,4},{7,5},{8,10},{9,11},{10,... | collective-permute-start | bytes 307208 | tf_op jit(solution)/shard_map/ppermute | solution.py:508
  28.3 13.9 %copy-start.2 = (f32[200,128]{1,0:T(8,128)}, f32[200,128]{1,0:T(8,128)S(1)}, u32[]{:S(2)}) copy-start(f32[200,128]{1,0:T(8,128)S(1)} %collective-permute-done.2.refs_1_) | copy-start | bytes 307204
  28.3 5.7 %collective-permute-start.6 = (f32[200,128]{1,0:T(8,128)S(1)}, f32[200,128]{1,0:T(8,128)S(1)}, u32[]{:S(2)}, u32[]{:S(2)}) collective-permute-start(f32[200,128]{1,0:T(8,128)S(1)} %collective-permute-done.2.refs_1_), channel_id=1, source_target_pairs={{0,4},{1,5},{2,6},{3,7},{4,0},{5,1},{6,2},{7,3},{8,12},{9,13},{10,... | collective-permute-start | bytes 307208 | tf_op jit(solution)/shard_map/ppermute | solution.py:508
  30.0 12.1 %copy-start.3 = (f32[200,128]{1,0:T(8,128)}, f32[200,128]{1,0:T(8,128)S(1)}, u32[]{:S(2)}) copy-start(f32[200,128]{1,0:T(8,128)S(1)} %collective-permute-done.9.refs_8_) | copy-start | bytes 307204
  30.0 4.7 %collective-permute-start.11 = (f32[200,128]{1,0:T(8,128)S(1)}, f32[200,128]{1,0:T(8,128)S(1)}, u32[]{:S(2)}, u32[]{:S(2)}) collective-permute-start(f32[200,128]{1,0:T(8,128)S(1)} %collective-permute-done.9.refs_8_), channel_id=1, source_target_pairs={{0,2},{1,3},{2,0},{3,1},{4,6},{5,7},{6,4},{7,5},{8,10},{9,11},{10,... | collective-permute-start | bytes 307208 | tf_op jit(solution)/shard_map/ppermute | solution.py:508
  31.8 10.4 %copy-start.4 = (f32[200,128]{1,0:T(8,128)}, f32[200,128]{1,0:T(8,128)S(1)}, u32[]{:S(2)}) copy-start(f32[200,128]{1,0:T(8,128)S(1)} %collective-permute-done.5.refs_4_) | copy-start | bytes 307204
  31.8 5.8 %collective-permute-start.13 = (f32[200,128]{1,0:T(8,128)S(1)}, f32[200,128]{1,0:T(8,128)S(1)}, u32[]{:S(2)}, u32[]{:S(2)}) collective-permute-start(f32[200,128]{1,0:T(8,128)S(1)} %collective-permute-done.5.refs_4_), channel_id=1, source_target_pairs={{0,8},{1,9},{2,10},{3,11},{4,12},{5,13},{6,14},{7,15},{8,0},{9,1},... | collective-permute-start | bytes 307208 | tf_op jit(solution)/shard_map/ppermute | solution.py:508
  32.3 5.3 %collective-permute-start.7 = (f32[200,128]{1,0:T(8,128)S(1)}, f32[200,128]{1,0:T(8,128)S(1)}, u32[]{:S(2)}, u32[]{:S(2)}) collective-permute-start(f32[200,128]{1,0:T(8,128)S(1)} %collective-permute-done.5.refs_4_), channel_id=1, source_target_pairs={{0,2},{1,3},{2,0},{3,1},{4,6},{5,7},{6,4},{7,5},{8,10},{9,11},{10,... | collective-permute-start | bytes 307208 | tf_op jit(solution)/shard_map/ppermute | solution.py:508
  32.3 9.9 %copy-start.5 = (f32[200,128]{1,0:T(8,128)}, f32[200,128]{1,0:T(8,128)S(1)}, u32[]{:S(2)}) copy-start(f32[200,128]{1,0:T(8,128)S(1)} %collective-permute-done.3.refs_2_) | copy-start | bytes 307204
  32.3 7.5 %collective-permute-start.10 = (f32[200,128]{1,0:T(8,128)S(1)}, f32[200,128]{1,0:T(8,128)S(1)}, u32[]{:S(2)}, u32[]{:S(2)}) collective-permute-start(f32[200,128]{1,0:T(8,128)S(1)} %collective-permute-done.2.refs_1_), channel_id=1, source_target_pairs={{0,8},{1,9},{2,10},{3,11},{4,12},{5,13},{6,14},{7,15},{8,0},{9,1},... | collective-permute-start | bytes 307208 | tf_op jit(solution)/shard_map/ppermute | solution.py:508
  33.9 8.3 %copy-start.6 = (f32[200,128]{1,0:T(8,128)}, f32[200,128]{1,0:T(8,128)S(1)}, u32[]{:S(2)}) copy-start(f32[200,128]{1,0:T(8,128)S(1)} %collective-permute-done.6.refs_5_) | copy-start | bytes 307204
  33.9 6.9 %collective-permute-start.14 = (f32[200,128]{1,0:T(8,128)S(1)}, f32[200,128]{1,0:T(8,128)S(1)}, u32[]{:S(2)}, u32[]{:S(2)}) collective-permute-start(f32[200,128]{1,0:T(8,128)S(1)} %collective-permute-done.6.refs_5_), channel_id=1, source_target_pairs={{0,8},{1,9},{2,10},{3,11},{4,12},{5,13},{6,14},{7,15},{8,0},{9,1},... | collective-permute-start | bytes 307208 | tf_op jit(solution)/shard_map/ppermute | solution.py:508
  34.8 7.5 %copy-start.7 = (f32[200,128]{1,0:T(8,128)}, f32[200,128]{1,0:T(8,128)S(1)}, u32[]{:S(2)}) copy-start(f32[200,128]{1,0:T(8,128)S(1)} %collective-permute-done.11.refs_10_) | copy-start | bytes 307204
  34.8 6.1 %collective-permute-start.4 = (f32[200,128]{1,0:T(8,128)S(1)}, f32[200,128]{1,0:T(8,128)S(1)}, u32[]{:S(2)}, u32[]{:S(2)}) collective-permute-start(f32[200,128]{1,0:T(8,128)S(1)} %collective-permute-done.2.refs_1_), channel_id=1, source_target_pairs={{0,2},{1,3},{2,0},{3,1},{4,6},{5,7},{6,4},{7,5},{8,10},{9,11},{10,... | collective-permute-start | bytes 307208 | tf_op jit(solution)/shard_map/ppermute | solution.py:508
  37.6 4.6 %copy-start.8 = (f32[200,128]{1,0:T(8,128)}, f32[200,128]{1,0:T(8,128)S(1)}, u32[]{:S(2)}) copy-start(f32[200,128]{1,0:T(8,128)S(1)} %collective-permute-done.13.refs_12_) | copy-start | bytes 307204
  37.6 3.5 %collective-permute-start.8 = (f32[200,128]{1,0:T(8,128)S(1)}, f32[200,128]{1,0:T(8,128)S(1)}, u32[]{:S(2)}, u32[]{:S(2)}) collective-permute-start(f32[200,128]{1,0:T(8,128)S(1)} %collective-permute-done.6.refs_5_), channel_id=1, source_target_pairs={{0,2},{1,3},{2,0},{3,1},{4,6},{5,7},{6,4},{7,5},{8,10},{9,11},{10,... | collective-permute-start | bytes 307208 | tf_op jit(solution)/shard_map/ppermute | solution.py:508
  37.6 4.6 %copy-start.9 = (f32[200,128]{1,0:T(8,128)}, f32[200,128]{1,0:T(8,128)S(1)}, u32[]{:S(2)}) copy-start(f32[200,128]{1,0:T(8,128)S(1)} %collective-permute-done.7.refs_6_) | copy-start | bytes 307204
  37.6 3.3 %collective-permute-start.15 = (f32[200,128]{1,0:T(8,128)S(1)}, f32[200,128]{1,0:T(8,128)S(1)}, u32[]{:S(2)}, u32[]{:S(2)}) collective-permute-start(f32[200,128]{1,0:T(8,128)S(1)} %collective-permute-done.13.refs_12_), channel_id=1, source_target_pairs={{0,2},{1,3},{2,0},{3,1},{4,6},{5,7},{6,4},{7,5},{8,10},{9,11},{10,... | collective-permute-start | bytes 307208 | tf_op jit(solution)/shard_map/ppermute | solution.py:508
  39.8 2.5 %copy-start.10 = (f32[200,128]{1,0:T(8,128)}, f32[200,128]{1,0:T(8,128)S(1)}, u32[]{:S(2)}) copy-start(f32[200,128]{1,0:T(8,128)S(1)} %collective-permute-done.10.refs_9_) | copy-start | bytes 307204
  39.8 1.3 %collective-permute-start.12 = (f32[200,128]{1,0:T(8,128)S(1)}, f32[200,128]{1,0:T(8,128)S(1)}, u32[]{:S(2)}, u32[]{:S(2)}) collective-permute-start(f32[200,128]{1,0:T(8,128)S(1)} %collective-permute-done.10.refs_9_), channel_id=1, source_target_pairs={{0,2},{1,3},{2,0},{3,1},{4,6},{5,7},{6,4},{7,5},{8,10},{9,11},{10,... | collective-permute-start | bytes 307208 | tf_op jit(solution)/shard_map/ppermute | solution.py:508
  40.9 1.4 %copy-start.11 = (f32[200,128]{1,0:T(8,128)}, f32[200,128]{1,0:T(8,128)S(1)}, u32[]{:S(2)}) copy-start(f32[200,128]{1,0:T(8,128)S(1)} %collective-permute-done.14.refs_13_) | copy-start | bytes 307204
  40.9 1.3 %collective-permute-start.16 = (f32[200,128]{1,0:T(8,128)S(1)}, f32[200,128]{1,0:T(8,128)S(1)}, u32[]{:S(2)}, u32[]{:S(2)}) collective-permute-start(f32[200,128]{1,0:T(8,128)S(1)} %collective-permute-done.14.refs_13_), channel_id=1, source_target_pairs={{0,2},{1,3},{2,0},{3,1},{4,6},{5,7},{6,4},{7,5},{8,10},{9,11},{10,... | collective-permute-start | bytes 307208 | tf_op jit(solution)/shard_map/ppermute | solution.py:508
  40.9 1.4 %copy-start.12 = (f32[200,128]{1,0:T(8,128)}, f32[200,128]{1,0:T(8,128)S(1)}, u32[]{:S(2)}) copy-start(f32[200,128]{1,0:T(8,128)S(1)} %collective-permute-done.4.refs_3_) | copy-start | bytes 307204
  40.9 1.4 %copy-start.14 = (f32[200,128]{1,0:T(8,128)}, f32[200,128]{1,0:T(8,128)S(1)}, u32[]{:S(2)}) copy-start(f32[200,128]{1,0:T(8,128)S(1)} %collective-permute-done.15.refs_14_) | copy-start | bytes 307204
  41.1 1.2 copy-start.15
  41.1 1.2 copy-start.13
  42.2 0.6 copy-start.16
where the time goes:
time: 125 us
  Pallas kernels  92.8 us (74%)
  waiting for transfers between devices  13.8 us (11%)
  starting transfers between devices  13.4 us (11%)
  other arithmetic  2.11 us (2%)
  local copies, waits for them, and re-layouts  1.85 us (1%)
    pallas_call x1, Pallas kernels, local(): pl.pallas_call(functools.partial(upper_kernel, nslots, blocks, lm_count),...  82 us
    ppermute x17, waiting for transfers between devices, swap(): return lax.ppermute(value, ('sub', 'lm'), pairs)  13.8 us
    ppermute x17, starting transfers between devices, swap(): return lax.ppermute(value, ('sub', 'lm'), pairs)  13.4 us
    pallas_call x1, Pallas kernels, local(): pl.pallas_call(bottom_kernel, out_shape=(payload, jax.ShapeDtypeStruct((E...  8.76 us
  transfers between devices with their start and end apart: 17, of which 8 were waited for; matrix products, arithmetic and copies ran while one was open for 0% of the time, Pallas kernels for 0%

commit v1 on v0

--- a/solution.py
+++ b/solution.py
@@ -137,7 +137,7 @@
         at = pl.ds(pl.multiple_of(c // 2 * 64, 64), 64)
         sum_ref[at, :] = sum_ref[at, :] + jnp.where(mine, cc, 0.0)
         index = jnp.where((lane8 == n) & (row8 == 0), c.astype(f32), index)
-        index = jnp.where((lane8 == n) & (row8 == 1), lm_ref[n].astype(f32), index)
+        index = jnp.where((lane8 == n) & (row8 == 1), (lm_ref[n] - NB).astype(f32), index)
     for k in range(blocks // 2):
         both = jnp.where(lane < 64, roll64(tops[2 * k]), tops[2 * k + 1])
         pay_ref[64 * k : 64 * k + 64, :] = both
@@ -518,7 +518,7 @@
         ]
     ).astype(jnp.int32)
     cams = camera_block[0]
-    lms = landmark_block[0] - NB
+    lms = landmark_block[0]
     payload = jax.ShapeDtypeStruct((48 * blocks + 8, 128), f32)
 
     pay, sums = pl.pallas_call(

time: 125 us -> 124 us (level)
  no operation moved by 1% of the time
where the time goes in v1:
time: 124 us
  Pallas kernels  92.9 us (75%)
  waiting for transfers between devices  13.8 us (11%)
  starting transfers between devices  13.4 us (11%)
  local copies, waits for them, and re-layouts  1.85 us (1%)
    pallas_call x1, Pallas kernels, local(): pl.pallas_call(functools.partial(upper_kernel, nslots, blocks, lm_count),...  82.1 us
    ppermute x17, waiting for transfers between devices, swap(): return lax.ppermute(value, ('sub', 'lm'), pairs)  13.8 us
    ppermute x17, starting transfers between devices, swap(): return lax.ppermute(value, ('sub', 'lm'), pairs)  13.4 us
    pallas_call x1, Pallas kernels, local(): pl.pallas_call(bottom_kernel, out_shape=(payload, jax.ShapeDtypeStruct((E...  8.76 us
  transfers between devices with their start and end apart: 17, of which 8 were waited for; matrix products, arithmetic and copies ran while one was open for 0% of the time, Pallas kernels for 0%

profile of v1, /device:TPU:0, one launch (start us, length us, event | category | flops | bytes accessed | tf_op | source)
XLA Modules:
  0.0 123.9 jit_solution(6393470623385233448)
XLA Ops:
  0.6 2.1 %shard_map.50 = (f32[200,128]{1,0:T(8,128)}, f32[320,128]{1,0:T(8,128)}) custom-call(s32[4]{0:T(128)} %bitcast.15, s32[4]{0:T(128)} %bitcast.17, bf16[4,384,128]{2,1,0:T(8,128)(2,1)} %bitcast.14), custom_call_target="tpu_custom_call" | custom-call | tf_op jit(solution)/shard_map/pallas_call | solution.py:524
  2.7 0.5 collective-permute-start
  3.2 1.2 collective-permute-done
  4.4 0.9 add.29.sum_a
  5.4 0.0 copy-start
  5.4 2.9 %collective-permute-start.1 = (f32[320,128]{1,0:T(8,128)S(1)}, f32[320,128]{1,0:T(8,128)S(1)}, u32[]{:S(2)}, u32[]{:S(2)}) collective-permute-start(f32[320,128]{1,0:T(8,128)S(1)} %add.29.sum_a), channel_id=1, source_target_pairs={{0,1},{1,0},{2,3},{3,2},{4,5},{5,4},{6,7},{7,6},{8,9},{9,8},{10,11... | collective-permute-start | bytes 491528 | tf_op jit(solution)/shard_map/ppermute | solution.py:508
  8.3 0.6 stack.23.info_ref
  8.9 3.9 %collective-permute-done.1.sum_b = f32[320,128]{1,0:T(8,128)S(1)} collective-permute-done((f32[320,128]{1,0:T(8,128)S(1)}, f32[320,128]{1,0:T(8,128)S(1)}, u32[]{:S(2)}, u32[]{:S(2)}) %collective-permute-start.1) | collective-permute-done | bytes 163872 | tf_op jit(solution)/shard_map/ppermute | solution.py:508
  12.8 0.0 copy-start.1
  12.8 0.0 copy-done
  12.8 0.7 copy-done.1
  13.5 8.8 %shard_map.51 = (f32[200,128]{1,0:T(8,128)}, f32[576,144]{1,0:T(8,128)}) custom-call(s32[6]{0:T(128)} %stack.23.info_ref, s32[4]{0:T(128)} %bitcast.16, f32[320,128]{1,0:T(8,128)} %copy-done, f32[320,128]{1,0:T(8,128)} %copy-done.1, f32[200,128]{1,0:T(8,128)} %get-tuple-element.9.pay_ref), custom_call_target="tpu_custom_call" | custom-call | tf_op jit(solution)/shard_map/pallas_call | solution.py:534
  22.2 1.7 %collective-permute-start.2 = (f32[200,128]{1,0:T(8,128)}, f32[200,128]{1,0:T(8,128)S(1)}, u32[]{:S(2)}, u32[]{:S(2)}) collective-permute-start(f32[200,128]{1,0:T(8,128)} %get-tuple-element.10.refs_0_), channel_id=1, source_target_pairs={{0,1},{1,0},{2,3},{3,2},{4,5},{5,4},{6,7},{7,6},{8,9},{9,8},{10,11... | collective-permute-start | bytes 307208 | tf_op jit(solution)/shard_map/ppermute | solution.py:508
  24.0 1.6 %collective-permute-start.9 = (f32[200,128]{1,0:T(8,128)}, f32[200,128]{1,0:T(8,128)S(1)}, u32[]{:S(2)}, u32[]{:S(2)}) collective-permute-start(f32[200,128]{1,0:T(8,128)} %get-tuple-element.10.refs_0_), channel_id=1, source_target_pairs={{0,8},{1,9},{2,10},{3,11},{4,12},{5,13},{6,14},{7,15},{8,0},{9,1},... | collective-permute-start | bytes 307208 | tf_op jit(solution)/shard_map/ppermute | solution.py:508
  25.5 1.5 %collective-permute-start.5 = (f32[200,128]{1,0:T(8,128)}, f32[200,128]{1,0:T(8,128)S(1)}, u32[]{:S(2)}, u32[]{:S(2)}) collective-permute-start(f32[200,128]{1,0:T(8,128)} %get-tuple-element.10.refs_0_), channel_id=1, source_target_pairs={{0,4},{1,5},{2,6},{3,7},{4,0},{5,1},{6,2},{7,3},{8,12},{9,13},{10,... | collective-permute-start | bytes 307208 | tf_op jit(solution)/shard_map/ppermute | solution.py:508
  27.1 0.0 collective-permute-start.3
  27.1 0.0 collective-permute-done.2.refs_1_
  27.1 0.0 copy-start.2
  27.1 1.8 %collective-permute-start.6 = (f32[200,128]{1,0:T(8,128)S(1)}, f32[200,128]{1,0:T(8,128)S(1)}, u32[]{:S(2)}, u32[]{:S(2)}) collective-permute-start(f32[200,128]{1,0:T(8,128)S(1)} %collective-permute-done.2.refs_1_), channel_id=1, source_target_pairs={{0,4},{1,5},{2,6},{3,7},{4,0},{5,1},{6,2},{7,3},{8,12},{9,13},{10,... | collective-permute-start | bytes 307208 | tf_op jit(solution)/shard_map/ppermute | solution.py:508
  28.9 0.0 collective-permute-done.9.refs_8_
  28.9 0.0 copy-start.3
  28.9 0.0 collective-permute-start.11
  28.9 1.8 %collective-permute-done.5.refs_4_ = f32[200,128]{1,0:T(8,128)S(1)} collective-permute-done((f32[200,128]{1,0:T(8,128)}, f32[200,128]{1,0:T(8,128)S(1)}, u32[]{:S(2)}, u32[]{:S(2)}) %collective-permute-start.5) | collective-permute-done | bytes 102432 | tf_op jit(solution)/shard_map/ppermute | solution.py:508
  30.6 0.0 copy-start.4
  30.6 0.5 collective-permute-start.13
  31.1 0.0 collective-permute-start.7
  31.1 0.0 collective-permute-done.3.refs_2_
  31.1 1.6 %collective-permute-start.10 = (f32[200,128]{1,0:T(8,128)S(1)}, f32[200,128]{1,0:T(8,128)S(1)}, u32[]{:S(2)}, u32[]{:S(2)}) collective-permute-start(f32[200,128]{1,0:T(8,128)S(1)} %collective-permute-done.2.refs_1_), channel_id=1, source_target_pairs={{0,8},{1,9},{2,10},{3,11},{4,12},{5,13},{6,14},{7,15},{8,0},{9,1},... | collective-permute-start | bytes 307208 | tf_op jit(solution)/shard_map/ppermute | solution.py:508
  32.7 0.0 collective-permute-done.6.refs_5_
  32.8 0.8 collective-permute-start.14
  33.6 0.0 collective-permute-done.11.refs_10_
  33.6 0.0 collective-permute-start.4
  33.6 2.8 %collective-permute-done.13.refs_12_ = f32[200,128]{1,0:T(8,128)S(1)} collective-permute-done((f32[200,128]{1,0:T(8,128)S(1)}, f32[200,128]{1,0:T(8,128)S(1)}, u32[]{:S(2)}, u32[]{:S(2)}) %collective-permute-start.13) | collective-permute-done | bytes 102432 | tf_op jit(solution)/shard_map/ppermute | solution.py:508
  36.4 0.0 collective-permute-start.8
  36.4 0.0 collective-permute-done.7.refs_6_
  36.4 0.0 copy-start.9
  36.4 0.5 collective-permute-start.15
  36.9 1.7 %collective-permute-done.10.refs_9_ = f32[200,128]{1,0:T(8,128)S(1)} collective-permute-done((f32[200,128]{1,0:T(8,128)S(1)}, f32[200,128]{1,0:T(8,128)S(1)}, u32[]{:S(2)}, u32[]{:S(2)}) %collective-permute-start.10) | collective-permute-done | bytes 102432 | tf_op jit(solution)/shard_map/ppermute | solution.py:508
  38.6 0.0 collective-permute-start.12
  38.6 1.1 collective-permute-done.14.refs_13_
  39.7 0.0 collective-permute-start.16
  39.7 0.0 collective-permute-done.4.refs_3_
  39.7 0.0 copy-start.12
  39.7 0.0 collective-permute-done.15.refs_14_
  39.7 0.0 copy-start.14
  39.7 0.2 collective-permute-done.12.refs_11_
  39.9 0.0 collective-permute-done.8.refs_7_
  39.9 1.1 collective-permute-done.16.refs_15_
  41.0 0.0 copy-done.2
  41.0 0.0 copy-done.3
  41.0 0.0 copy-done.4
  41.0 0.0 copy-done.5
  41.0 0.0 copy-done.6
  41.0 0.0 copy-done.7
  41.0 0.0 copy-done.8
  41.1 0.0 copy-done.9
  41.1 0.0 copy-done.10
  41.1 0.0 copy-done.11
  41.1 0.0 copy-done.12
  41.1 0.0 copy-done.14
  41.1 0.0 copy-done.15
  41.1 0.0 copy-done.13
  41.1 0.5 copy-done.16
  41.6 82.1 %shard_map.52 = (f32[3,576,252]{2,1,0:T(8,128)}, f32[2,36,1,1152]{3,2,1,0:T(1,128)}) custom-call(s32[6]{0:T(128)} %stack.23.info_ref, f32[200,128]{1,0:T(8,128)} %get-tuple-element.10.refs_0_, f32[200,128]{1,0:T(8,128)} %copy-done.2, f32[200,128]{1,0:T(8,128)} %copy-done.5, f32[200,128]{1,0:T(8,128)} %copy-done.12, f32[200,128]{1,0:T(8,128)} %copy-done.4, ...), custom_call_target="tpu_custom_call" | custom-call | tf_op jit(solution)/shard_map/pallas_call | solution.py:548
  (9 shorter events, 0.0 us)
Async XLA Ops:
  2.7 1.7 %collective-permute-start = (f32[320,128]{1,0:T(8,128)}, f32[320,128]{1,0:T(8,128)S(1)}, u32[]{:S(2)}, u32[]{:S(2)}) collective-permute-start(f32[320,128]{1,0:T(8,128)} %get-tuple-element.8), channel_id=1, source_target_pairs={{0,2},{1,3},{2,0},{3,1},{4,6},{5,7},{6,4},{7,5},{8,10},{9,11},{10,... | collective-permute-start | bytes 491528 | tf_op jit(solution)/shard_map/ppermute | solution.py:508
  5.4 7.4 %copy-start = (f32[320,128]{1,0:T(8,128)}, f32[320,128]{1,0:T(8,128)S(1)}, u32[]{:S(2)}) copy-start(f32[320,128]{1,0:T(8,128)S(1)} %add.29.sum_a) | copy-start | bytes 491524
  5.4 7.4 %collective-permute-start.1 = (f32[320,128]{1,0:T(8,128)S(1)}, f32[320,128]{1,0:T(8,128)S(1)}, u32[]{:S(2)}, u32[]{:S(2)}) collective-permute-start(f32[320,128]{1,0:T(8,128)S(1)} %add.29.sum_a), channel_id=1, source_target_pairs={{0,1},{1,0},{2,3},{3,2},{4,5},{5,4},{6,7},{7,6},{8,9},{9,8},{10,11... | collective-permute-start | bytes 491528 | tf_op jit(solution)/shard_map/ppermute | solution.py:508
  12.8 0.7 copy-start.1
  22.2 4.9 %collective-permute-start.2 = (f32[200,128]{1,0:T(8,128)}, f32[200,128]{1,0:T(8,128)S(1)}, u32[]{:S(2)}, u32[]{:S(2)}) collective-permute-start(f32[200,128]{1,0:T(8,128)} %get-tuple-element.10.refs_0_), channel_id=1, source_target_pairs={{0,1},{1,0},{2,3},{3,2},{4,5},{5,4},{6,7},{7,6},{8,9},{9,8},{10,11... | collective-permute-start | bytes 307208 | tf_op jit(solution)/shard_map/ppermute | solution.py:508
  24.0 4.9 %collective-permute-start.9 = (f32[200,128]{1,0:T(8,128)}, f32[200,128]{1,0:T(8,128)S(1)}, u32[]{:S(2)}, u32[]{:S(2)}) collective-permute-start(f32[200,128]{1,0:T(8,128)} %get-tuple-element.10.refs_0_), channel_id=1, source_target_pairs={{0,8},{1,9},{2,10},{3,11},{4,12},{5,13},{6,14},{7,15},{8,0},{9,1},... | collective-permute-start | bytes 307208 | tf_op jit(solution)/shard_map/ppermute | solution.py:508
  25.5 5.1 %collective-permute-start.5 = (f32[200,128]{1,0:T(8,128)}, f32[200,128]{1,0:T(8,128)S(1)}, u32[]{:S(2)}, u32[]{:S(2)}) collective-permute-start(f32[200,128]{1,0:T(8,128)} %get-tuple-element.10.refs_0_), channel_id=1, source_target_pairs={{0,4},{1,5},{2,6},{3,7},{4,0},{5,1},{6,2},{7,3},{8,12},{9,13},{10,... | collective-permute-start | bytes 307208 | tf_op jit(solution)/shard_map/ppermute | solution.py:508
  27.1 4.0 %collective-permute-start.3 = (f32[200,128]{1,0:T(8,128)}, f32[200,128]{1,0:T(8,128)S(1)}, u32[]{:S(2)}, u32[]{:S(2)}) collective-permute-start(f32[200,128]{1,0:T(8,128)} %get-tuple-element.10.refs_0_), channel_id=1, source_target_pairs={{0,2},{1,3},{2,0},{3,1},{4,6},{5,7},{6,4},{7,5},{8,10},{9,11},{10,... | collective-permute-start | bytes 307208 | tf_op jit(solution)/shard_map/ppermute | solution.py:508
  27.1 13.9 %copy-start.2 = (f32[200,128]{1,0:T(8,128)}, f32[200,128]{1,0:T(8,128)S(1)}, u32[]{:S(2)}) copy-start(f32[200,128]{1,0:T(8,128)S(1)} %collective-permute-done.2.refs_1_) | copy-start | bytes 307204
  27.1 5.7 %collective-permute-start.6 = (f32[200,128]{1,0:T(8,128)S(1)}, f32[200,128]{1,0:T(8,128)S(1)}, u32[]{:S(2)}, u32[]{:S(2)}) collective-permute-start(f32[200,128]{1,0:T(8,128)S(1)} %collective-permute-done.2.refs_1_), channel_id=1, source_target_pairs={{0,4},{1,5},{2,6},{3,7},{4,0},{5,1},{6,2},{7,3},{8,12},{9,13},{10,... | collective-permute-start | bytes 307208 | tf_op jit(solution)/shard_map/ppermute | solution.py:508
  28.9 12.1 %copy-start.3 = (f32[200,128]{1,0:T(8,128)}, f32[200,128]{1,0:T(8,128)S(1)}, u32[]{:S(2)}) copy-start(f32[200,128]{1,0:T(8,128)S(1)} %collective-permute-done.9.refs_8_) | copy-start | bytes 307204
  28.9 4.7 %collective-permute-start.11 = (f32[200,128]{1,0:T(8,128)S(1)}, f32[200,128]{1,0:T(8,128)S(1)}, u32[]{:S(2)}, u32[]{:S(2)}) collective-permute-start(f32[200,128]{1,0:T(8,128)S(1)} %collective-permute-done.9.refs_8_), channel_id=1, source_target_pairs={{0,2},{1,3},{2,0},{3,1},{4,6},{5,7},{6,4},{7,5},{8,10},{9,11},{10,... | collective-permute-start | bytes 307208 | tf_op jit(solution)/shard_map/ppermute | solution.py:508
  30.6 10.4 %copy-start.4 = (f32[200,128]{1,0:T(8,128)}, f32[200,128]{1,0:T(8,128)S(1)}, u32[]{:S(2)}) copy-start(f32[200,128]{1,0:T(8,128)S(1)} %collective-permute-done.5.refs_4_) | copy-start | bytes 307204
  30.6 5.8 %collective-permute-start.13 = (f32[200,128]{1,0:T(8,128)S(1)}, f32[200,128]{1,0:T(8,128)S(1)}, u32[]{:S(2)}, u32[]{:S(2)}) collective-permute-start(f32[200,128]{1,0:T(8,128)S(1)} %collective-permute-done.5.refs_4_), channel_id=1, source_target_pairs={{0,8},{1,9},{2,10},{3,11},{4,12},{5,13},{6,14},{7,15},{8,0},{9,1},... | collective-permute-start | bytes 307208 | tf_op jit(solution)/shard_map/ppermute | solution.py:508
  31.1 5.3 %collective-permute-start.7 = (f32[200,128]{1,0:T(8,128)S(1)}, f32[200,128]{1,0:T(8,128)S(1)}, u32[]{:S(2)}, u32[]{:S(2)}) collective-permute-start(f32[200,128]{1,0:T(8,128)S(1)} %collective-permute-done.5.refs_4_), channel_id=1, source_target_pairs={{0,2},{1,3},{2,0},{3,1},{4,6},{5,7},{6,4},{7,5},{8,10},{9,11},{10,... | collective-permute-start | bytes 307208 | tf_op jit(solution)/shard_map/ppermute | solution.py:508
  31.1 9.9 %copy-start.5 = (f32[200,128]{1,0:T(8,128)}, f32[200,128]{1,0:T(8,128)S(1)}, u32[]{:S(2)}) copy-start(f32[200,128]{1,0:T(8,128)S(1)} %collective-permute-done.3.refs_2_) | copy-start | bytes 307204
  31.1 7.5 %collective-permute-start.10 = (f32[200,128]{1,0:T(8,128)S(1)}, f32[200,128]{1,0:T(8,128)S(1)}, u32[]{:S(2)}, u32[]{:S(2)}) collective-permute-start(f32[200,128]{1,0:T(8,128)S(1)} %collective-permute-done.2.refs_1_), channel_id=1, source_target_pairs={{0,8},{1,9},{2,10},{3,11},{4,12},{5,13},{6,14},{7,15},{8,0},{9,1},... | collective-permute-start | bytes 307208 | tf_op jit(solution)/shard_map/ppermute | solution.py:508
  32.8 8.3 %copy-start.6 = (f32[200,128]{1,0:T(8,128)}, f32[200,128]{1,0:T(8,128)S(1)}, u32[]{:S(2)}) copy-start(f32[200,128]{1,0:T(8,128)S(1)} %collective-permute-done.6.refs_5_) | copy-start | bytes 307204
  32.8 6.9 %collective-permute-start.14 = (f32[200,128]{1,0:T(8,128)S(1)}, f32[200,128]{1,0:T(8,128)S(1)}, u32[]{:S(2)}, u32[]{:S(2)}) collective-permute-start(f32[200,128]{1,0:T(8,128)S(1)} %collective-permute-done.6.refs_5_), channel_id=1, source_target_pairs={{0,8},{1,9},{2,10},{3,11},{4,12},{5,13},{6,14},{7,15},{8,0},{9,1},... | collective-permute-start | bytes 307208 | tf_op jit(solution)/shard_map/ppermute | solution.py:508
  33.6 7.5 %copy-start.7 = (f32[200,128]{1,0:T(8,128)}, f32[200,128]{1,0:T(8,128)S(1)}, u32[]{:S(2)}) copy-start(f32[200,128]{1,0:T(8,128)S(1)} %collective-permute-done.11.refs_10_) | copy-start | bytes 307204
  33.6 6.1 %collective-permute-start.4 = (f32[200,128]{1,0:T(8,128)S(1)}, f32[200,128]{1,0:T(8,128)S(1)}, u32[]{:S(2)}, u32[]{:S(2)}) collective-permute-start(f32[200,128]{1,0:T(8,128)S(1)} %collective-permute-done.2.refs_1_), channel_id=1, source_target_pairs={{0,2},{1,3},{2,0},{3,1},{4,6},{5,7},{6,4},{7,5},{8,10},{9,11},{10,... | collective-permute-start | bytes 307208 | tf_op jit(solution)/shard_map/ppermute | solution.py:508
  36.4 4.6 %copy-start.8 = (f32[200,128]{1,0:T(8,128)}, f32[200,128]{1,0:T(8,128)S(1)}, u32[]{:S(2)}) copy-start(f32[200,128]{1,0:T(8,128)S(1)} %collective-permute-done.13.refs_12_) | copy-start | bytes 307204
  36.4 3.5 %collective-permute-start.8 = (f32[200,128]{1,0:T(8,128)S(1)}, f32[200,128]{1,0:T(8,128)S(1)}, u32[]{:S(2)}, u32[]{:S(2)}) collective-permute-start(f32[200,128]{1,0:T(8,128)S(1)} %collective-permute-done.6.refs_5_), channel_id=1, source_target_pairs={{0,2},{1,3},{2,0},{3,1},{4,6},{5,7},{6,4},{7,5},{8,10},{9,11},{10,... | collective-permute-start | bytes 307208 | tf_op jit(solution)/shard_map/ppermute | solution.py:508
  36.4 4.6 %copy-start.9 = (f32[200,128]{1,0:T(8,128)}, f32[200,128]{1,0:T(8,128)S(1)}, u32[]{:S(2)}) copy-start(f32[200,128]{1,0:T(8,128)S(1)} %collective-permute-done.7.refs_6_) | copy-start | bytes 307204
  36.4 3.3 %collective-permute-start.15 = (f32[200,128]{1,0:T(8,128)S(1)}, f32[200,128]{1,0:T(8,128)S(1)}, u32[]{:S(2)}, u32[]{:S(2)}) collective-permute-start(f32[200,128]{1,0:T(8,128)S(1)} %collective-permute-done.13.refs_12_), channel_id=1, source_target_pairs={{0,2},{1,3},{2,0},{3,1},{4,6},{5,7},{6,4},{7,5},{8,10},{9,11},{10,... | collective-permute-start | bytes 307208 | tf_op jit(solution)/shard_map/ppermute | solution.py:508
  38.6 2.5 %copy-start.10 = (f32[200,128]{1,0:T(8,128)}, f32[200,128]{1,0:T(8,128)S(1)}, u32[]{:S(2)}) copy-start(f32[200,128]{1,0:T(8,128)S(1)} %collective-permute-done.10.refs_9_) | copy-start | bytes 307204
  38.6 1.3 %collective-permute-start.12 = (f32[200,128]{1,0:T(8,128)S(1)}, f32[200,128]{1,0:T(8,128)S(1)}, u32[]{:S(2)}, u32[]{:S(2)}) collective-permute-start(f32[200,128]{1,0:T(8,128)S(1)} %collective-permute-done.10.refs_9_), channel_id=1, source_target_pairs={{0,2},{1,3},{2,0},{3,1},{4,6},{5,7},{6,4},{7,5},{8,10},{9,11},{10,... | collective-permute-start | bytes 307208 | tf_op jit(solution)/shard_map/ppermute | solution.py:508
  39.7 1.4 %copy-start.11 = (f32[200,128]{1,0:T(8,128)}, f32[200,128]{1,0:T(8,128)S(1)}, u32[]{:S(2)}) copy-start(f32[200,128]{1,0:T(8,128)S(1)} %collective-permute-done.14.refs_13_) | copy-start | bytes 307204
  39.7 1.3 %collective-permute-start.16 = (f32[200,128]{1,0:T(8,128)S(1)}, f32[200,128]{1,0:T(8,128)S(1)}, u32[]{:S(2)}, u32[]{:S(2)}) collective-permute-start(f32[200,128]{1,0:T(8,128)S(1)} %collective-permute-done.14.refs_13_), channel_id=1, source_target_pairs={{0,2},{1,3},{2,0},{3,1},{4,6},{5,7},{6,4},{7,5},{8,10},{9,11},{10,... | collective-permute-start | bytes 307208 | tf_op jit(solution)/shard_map/ppermute | solution.py:508
  39.7 1.4 %copy-start.12 = (f32[200,128]{1,0:T(8,128)}, f32[200,128]{1,0:T(8,128)S(1)}, u32[]{:S(2)}) copy-start(f32[200,128]{1,0:T(8,128)S(1)} %collective-permute-done.4.refs_3_) | copy-start | bytes 307204
  39.7 1.4 %copy-start.14 = (f32[200,128]{1,0:T(8,128)}, f32[200,128]{1,0:T(8,128)S(1)}, u32[]{:S(2)}) copy-start(f32[200,128]{1,0:T(8,128)S(1)} %collective-permute-done.15.refs_14_) | copy-start | bytes 307204
  39.9 1.2 copy-start.15
  39.9 1.2 copy-start.13
  41.0 0.6 copy-start.16
